TPU v7x, 512 devices: a whole 4x8x8 slice. The times are simulated.
512 devices in a mesh: grp: 16 (over z, x_hi), blk: 32 (over x_lo, y, core).
Axes of the slice: x: 4 (x_hi: 2, x_lo: 2; x = x_hi * 2 + x_lo), y: 8, z: 8, core: 2. Of those that a mesh axis runs over, the one named last changes fastest.
Arguments:
- ao_ints: bfloat16 [128, 1504, 1504], P('grp', 'blk'), may hold values from -6 to 6
- v_coeff: bfloat16 [1504, 1344], P(None, 'blk'), may hold values from -0.15625 to 0.15625
- batch_start: int32 [16], replicated, may hold values from 0 to 1496, as said below
- owner_map: int32 [32], replicated, may hold values from 0 to 31, each once
Outputs:
- slab: bfloat16 [128, 1344, 1344], P(None, 'blk', 'grp')
Inputs may be any that keep to these rules, and one draw needn't show every extreme that they name: `batch_start`: distinct multiples of 8; one entry is 0 and one is 1496. `owner_map`: each block number appears once.
All inputs are finite; a program needn't handle non-finite values.
Results may differ from a plain program's by a relative error of at most 0.0049.
Values may be sent and summed in bfloat16 or wider, within the bound.
No kernel may reach another device: no remote copies, remote signals or barrier semaphores. Data moves between devices by JAX's collectives and lax.ppermute only.
A program may use at most 64 MiB of HBM per device.

v0:
```python
import jax
import jax.numpy as jnp
from jax import lax
from jax.sharding import PartitionSpec as P


def in_blocks(x, dim, size):
    before, after = (x.shape[:dim], x.shape[dim + 1 :])
    return jnp.moveaxis(x.reshape(*before, size, -1, *after), dim, 0)


def edges_of(length, count):
    unit = 8 if length >= 8 * count else 1
    return [length // unit * k // count * unit for k in range(1, count)]


def joined_along(pieces, dim):
    pieces = jnp.moveaxis(pieces, 0, dim)
    lengths = pieces.shape
    return pieces.reshape(*lengths[:dim], lengths[dim] * lengths[dim + 1], *lengths[dim + 2 :])


def several_exchanges(x, axis, pieces, split_dim, concat_dim):
    blocks = in_blocks(x, split_dim, lax.axis_size(axis))
    split_at = max(range(1, max(2, blocks.ndim - 1)), key=lambda d: blocks.shape[d])
    gathered = []
    for section in jnp.split(blocks, edges_of(blocks.shape[split_at], pieces), axis=split_at):
        if section.size:
            gathered.append(lax.all_to_all(section, axis, split_axis=0, concat_axis=0, tiled=True))
    return joined_along(jnp.concatenate(gathered, axis=split_at), concat_dim)


def local(ao_ints, v_coeff, batch_start, owner_map):
    sig_rows, lam_rows, ao_count = ao_ints.shape
    ints_flat = ao_ints.reshape(sig_rows * lam_rows, ao_count)
    v_whole = lax.all_gather(v_coeff, "blk", axis=1, tiled=True)
    half_done = jnp.dot(ints_flat, v_whole, preferred_element_type=jnp.float32).astype(jnp.bfloat16)
    half_done = half_done.reshape(sig_rows, lam_rows, -1)
    owned_rows = lax.all_to_all(half_done, "blk", split_axis=2, concat_axis=1, tiled=True)
    third_done = lax.dot_general(
        owned_rows, v_whole, (((1,), (0,)), ((), ())), preferred_element_type=jnp.float32
    ).astype(jnp.bfloat16)
    a_local = third_done.shape[1]
    block_count = owner_map.shape[0]
    block_width = third_done.shape[2] // block_count
    blocked = third_done.reshape(sig_rows, a_local, block_count, block_width)
    ordered = jnp.take(blocked, owner_map, axis=2).reshape(
        sig_rows, a_local, block_count * block_width
    )
    group_count = batch_start.shape[0]
    group_ids = jnp.arange(group_count, dtype=jnp.int32)
    rank = jnp.sum((batch_start[None, :] < batch_start[:, None]).astype(jnp.int32), axis=1)
    source = jnp.sum(
        group_ids[None, :] * (rank[None, :] == group_ids[:, None]).astype(jnp.int32), axis=1
    )
    received = several_exchanges(ordered, "grp", 2, 2, 0)
    item_count = received.shape[1]
    own_width = received.shape[2]
    grouped = received.reshape(group_count, sig_rows, item_count, own_width)
    return jnp.take(grouped, source, axis=0).reshape(group_count * sig_rows, item_count, own_width)


def solution(mesh):
    return jax.shard_map(
        local,
        mesh=mesh,
        in_specs=(P("grp", "blk", None), P(None, "blk"), P(), P()),
        out_specs=P(None, "blk", "grp"),
        check_vma=False,
    )
```

profile of v0, /device:TPU:8, one launch (start us, length us, event | category | flops | bytes accessed | tf_op | source)
XLA Modules:
  0.0 247.0 jit_solution(10376196617440628879)
XLA Ops:
  6.5 0.0 all-gather.3.cloned.1.call-start
  6.5 0.7 all-gather.3.cloned.1.call-update
  7.3 1.6 copy.37
  8.9 0.5 reshape.43
  9.4 73.7 %all-gather.3.cloned.1.call-done = bf16[32,42,1504]{2,1,0:T(8,128)(2,1)} async-done(((bf16[1,42,1504]{2,1,0:T(8,128)(2,1)}), bf16[32,42,1504]{2,1,0:T(8,128)(2,1)}) %all-gather.3.cloned.1.call-update) | async-done | bytes 4042768 | tf_op jit(solution)/shard_map/all_gather | solution.py:36
  83.1 7.5 %reshape.64 = bf16[1344,1504]{1,0:T(8,128)(2,1)} reshape(bf16[32,42,1504]{2,1,0:T(8,128)(2,1)} %all-gather.3.cloned.1.call-done) | data formatting | bytes 8085504
  90.6 5.5 %convolution_convert_fusion.1 = bf16[376,1344]{0,1:T(8,128)(2,1)} fusion(bf16[376,1504]{1,0:T(8,128)(2,1)S(1)} %reshape.43, bf16[1344,1504]{1,0:T(8,128)(2,1)} %reshape.64), kind=kOutput, calls=%fused_computation.3 | convolution fusion | flops 1520580096 | bytes 6184448 | tf_op jit(solution)/shard_map/dot_general | solution.py:37
  96.1 3.8 %reshape.66 = bf16[8,47,1344]{1,0,2:T(8,128)(2,1)S(1)} reshape(bf16[376,1344]{0,1:T(8,128)(2,1)} %convolution_convert_fusion.1) | data formatting | bytes 2021376 | tf_op jit(solution)/shard_map/reshape | solution.py:38
  99.9 4.9 %reshape.70 = bf16[32,2,7896]{2,1,0:T(2,128)(2,1)} reshape(bf16[1344,8,47]{2,1,0:T(8,128)(2,1)S(1)} %bitcast.31) | data formatting | bytes 2021376
  104.8 0.0 copy-start
  104.8 7.7 %all-to-all-start = ((bf16[32,2,7896]{2,1,0:T(2,128)(2,1)}), bf16[32,2,7896]{2,1,0:T(2,128)(2,1)}, u32[]{:S(2)}, u32[]{:S(2)}) async-start(bf16[32,2,7896]{2,1,0:T(2,128)(2,1)} %reshape.70), calls=%async_computation | async-start | bytes 2031616 | tf_op jit(solution)/shard_map/all_to_all | solution.py:39
  112.6 0.0 copy-done
  112.6 0.1 broadcast_in_dim.40
  112.7 0.1 broadcast_in_dim.41
  112.8 0.1 broadcast_in_dim.42
  112.9 7.5 %reshape.65 = bf16[1344,1504,1]{1,0,2:T(8,128)(2,1)} reshape(bf16[32,42,1504]{2,1,0:T(8,128)(2,1)} %all-gather.3.cloned.1.call-done) | data formatting | bytes 8085504
  120.3 20.5 %all-to-all-done = bf16[32,2,7896]{2,1,0:T(2,128)(2,1)} async-done(((bf16[32,2,7896]{2,1,0:T(2,128)(2,1)}), bf16[32,2,7896]{2,1,0:T(2,128)(2,1)}, u32[]{:S(2)}, u32[]{:S(2)}) %all-to-all-start) | async-done | bytes 1010720 | tf_op jit(solution)/shard_map/all_to_all | solution.py:39
  140.9 5.5 %reshape.71 = bf16[1344,8,47]{2,1,0:T(8,128)(2,1)S(1)} reshape(bf16[32,2,7896]{2,1,0:T(2,128)(2,1)} %all-to-all-done) | data formatting | bytes 2021376
  146.4 2.3 copy.51
  148.7 5.7 %reshape.67 = bf16[8,1504,42]{1,2,0:T(8,128)(2,1)S(1)} reshape(bf16[8,32,47,42]{2,1,3,0:T(8,128)(2,1)} %copy.51) | data formatting | bytes 2021376 | tf_op jit(solution)/shard_map/all_to_all | solution.py:39
  154.3 4.2 %convolution_convert_fusion = bf16[8,42,1344]{2,1,0:T(8,128)(2,1)S(1)} fusion(bf16[8,1504,42]{1,2,0:T(8,128)(2,1)S(1)} %reshape.67, bf16[1344,1504,1]{1,0,2:T(8,128)(2,1)} %reshape.65), kind=kOutput, calls=%fused_computation.2 | convolution fusion | flops 1358816256 | bytes 5956608 | tf_op jit(solution)/shard_map/dot_general | solution.py:40
  158.5 8.9 %reshape.69 = bf16[8,42,32,42]{3,2,1,0:T(8,128)(2,1)} reshape(bf16[8,42,1344]{2,1,0:T(8,128)(2,1)S(1)} %convolution_convert_fusion) | data formatting | bytes 1806336 | tf_op jit(solution)/shard_map/reshape | solution.py:46
  167.5 5.0 %copy.44 = bf16[8,42,32,42]{3,0,2,1:T(8,128)(2,1)S(1)} copy(bf16[8,42,32,42]{3,2,1,0:T(8,128)(2,1)} %reshape.69) | data formatting | bytes 1806336 | tf_op jit(solution)/shard_map/reshape | solution.py:46
  172.4 3.0 %gather_fusion = bf16[32,8,42,42]{3,1,2,0:T(8,128)(2,1)} fusion(bf16[8,42,32,42]{3,0,2,1:T(8,128)(2,1)S(1)} %copy.44, s32[1024]{0:T(1024)S(1)} %pad_clamp_fusion.1), kind=kCustom, calls=%fused_computation | custom fusion | bytes 1806464 | tf_op jit(solution)/shard_map/jit(_take)/gather | solution.py:47
  175.4 2.5 %copy.45 = bf16[8,42,32,42]{3,2,1,0:T(8,128)(2,1)S(1)} copy(bf16[8,42,32,42]{3,0,1,2:T(8,128)(2,1)} %bitcast.30) | data formatting | bytes 1806336 | tf_op jit(solution)/shard_map/jit(_take)/gather | solution.py:47
  177.9 2.4 gather.13
  180.3 1.8 fusion
  182.1 0.8 split.8
  182.9 9.5 %all-to-all-start.1 = ((bf16[16,8,16,84]{3,1,2,0:T(8,128)(2,1)}), bf16[16,8,16,84]{3,1,2,0:T(8,128)(2,1)S(1)}, u32[]{:S(2)}, u32[]{:S(2)}) async-start(bf16[16,8,16,84]{3,1,2,0:T(8,128)(2,1)} %split.8), calls=%async_computation.1 | async-start | bytes 1048576 | tf_op jit(solution)/shard_map/all_to_all | solution.py:29
  192.4 0.0 copy-start.1
  192.4 1.0 split.9
  193.4 16.7 %all-to-all-done.1 = bf16[16,8,16,84]{3,1,2,0:T(8,128)(2,1)S(1)} async-done(((bf16[16,8,16,84]{3,1,2,0:T(8,128)(2,1)}), bf16[16,8,16,84]{3,1,2,0:T(8,128)(2,1)S(1)}, u32[]{:S(2)}, u32[]{:S(2)}) %all-to-all-start.1) | async-done | bytes 344096 | tf_op jit(solution)/shard_map/all_to_all | solution.py:29
  210.1 3.6 %all-to-all-start.2 = ((bf16[16,8,26,84]{3,1,2,0:T(8,128)(2,1)}), bf16[16,8,26,84]{3,1,2,0:T(8,128)(2,1)S(1)}, u32[]{:S(2)}, u32[]{:S(2)}) async-start(bf16[16,8,26,84]{3,1,2,0:T(8,128)(2,1)} %split.9), calls=%async_computation.2 | async-start | bytes 1703936 | tf_op jit(solution)/shard_map/all_to_all | solution.py:29
  213.7 0.0 copy-done.1
  213.8 0.2 convert_reduce_fusion
  213.9 0.1 select_reduce_fusion
  214.1 0.1 broadcast_in_dim.37
  214.1 0.1 broadcast_in_dim.38
  214.3 23.0 %all-to-all-done.2 = bf16[16,8,26,84]{3,1,2,0:T(8,128)(2,1)S(1)} async-done(((bf16[16,8,26,84]{3,1,2,0:T(8,128)(2,1)}), bf16[16,8,26,84]{3,1,2,0:T(8,128)(2,1)S(1)}, u32[]{:S(2)}, u32[]{:S(2)}) %all-to-all-start.2) | async-done | bytes 559136 | tf_op jit(solution)/shard_map/all_to_all | solution.py:29
  237.3 0.3 pad_maximum_fusion
  237.6 0.8 gather_fusion.1
  238.4 0.2 bitcast_select_fusion
  238.6 1.5 copy.48
  (6 shorter events, 0.0 us)
Async XLA Ops:
  6.5 76.6 %all-gather.3.cloned.1.call-start = ((), (), s32[]{:S(2)}) async-start(), calls=%async_computation.3 | async-start | bytes 4866048 | tf_op jit(solution)/shard_map/all_gather | solution.py:36
  104.8 7.7 %copy-start = (s32[32]{0:T(128)S(1)}, s32[32]{0:T(128)}, u32[]{:S(2)}) copy-start(s32[32]{0:T(128)} %param.7) | copy-start | bytes 388
  104.8 36.0 %all-to-all-start = ((bf16[32,2,7896]{2,1,0:T(2,128)(2,1)}), bf16[32,2,7896]{2,1,0:T(2,128)(2,1)}, u32[]{:S(2)}, u32[]{:S(2)}) async-start(bf16[32,2,7896]{2,1,0:T(2,128)(2,1)} %reshape.70), calls=%async_computation | async-start | bytes 2031616 | tf_op jit(solution)/shard_map/all_to_all | solution.py:39
  182.9 27.2 %all-to-all-start.1 = ((bf16[16,8,16,84]{3,1,2,0:T(8,128)(2,1)}), bf16[16,8,16,84]{3,1,2,0:T(8,128)(2,1)S(1)}, u32[]{:S(2)}, u32[]{:S(2)}) async-start(bf16[16,8,16,84]{3,1,2,0:T(8,128)(2,1)} %split.8), calls=%async_computation.1 | async-start | bytes 1048576 | tf_op jit(solution)/shard_map/all_to_all | solution.py:29
  192.4 21.3 %copy-start.1 = (s32[16]{0:T(128)S(1)}, s32[16]{0:T(128)}, u32[]{:S(2)}) copy-start(s32[16]{0:T(128)} %param.6) | copy-start | bytes 196
  210.1 27.2 %all-to-all-start.2 = ((bf16[16,8,26,84]{3,1,2,0:T(8,128)(2,1)}), bf16[16,8,26,84]{3,1,2,0:T(8,128)(2,1)S(1)}, u32[]{:S(2)}, u32[]{:S(2)}) async-start(bf16[16,8,26,84]{3,1,2,0:T(8,128)(2,1)} %split.9), calls=%async_computation.2 | async-start | bytes 1703936 | tf_op jit(solution)/shard_map/all_to_all | solution.py:29
Sparse Core Ops, SparseCore 0:
  9.5 73.5 all-gather.2
where the time goes:
time: 248 us; the launch traced here: 247 us
  waiting for transfers between devices  135 us (54%)
  local copies, waits for them, and re-layouts  65.6 us (26%)
  starting transfers between devices  20.8 us (8%)
  between operations  13.6 us (5%)
  matrix products  9.71 us (4%)
  other arithmetic  2.65 us (1%)
    all_gather x1, waiting for transfers between devices, local(): v_whole = lax.all_gather(v_coeff, 'blk', axis=1, tiled=True)  73.7 us
    all_to_all x2, waiting for transfers between devices, several_exchanges(): lax.all_to_all(section, axis, split_axis=0, concat_axis=0, tiled=True)  39.7 us
    unnamed x9, local copies, waits for them, and re-layouts  27 us
    all_to_all x1, waiting for transfers between devices, local(): lax.all_to_all(half_done, 'blk', split_axis=2, concat_axis=1, tiled=True)  20.5 us
    reshape x2, local copies, waits for them, and re-layouts, local(): blocked = third_done.reshape(sig_rows, a_local, block_count, block_width)  13.9 us
    all_to_all x2, starting transfers between devices, several_exchanges(): lax.all_to_all(section, axis, split_axis=0, concat_axis=0, tiled=True)  13.1 us
    all_to_all x2, local copies, waits for them, and re-layouts, local(): lax.all_to_all(half_done, 'blk', split_axis=2, concat_axis=1, tiled=True)  7.93 us
    gather x3, local copies, waits for them, and re-layouts, local(): jnp.take(blocked, owner_map, axis=2)  7.84 us
  transfers between devices with their start and end apart: 4, of which 4 were waited for; matrix products, arithmetic and copies ran while one was open for 5% of the time, Pallas kernels for 0%

commit v1 on v0

--- a/solution.py
+++ b/solution.py
@@ -33,7 +33,10 @@
 def local(ao_ints, v_coeff, batch_start, owner_map):
     sig_rows, lam_rows, ao_count = ao_ints.shape
     ints_flat = ao_ints.reshape(sig_rows * lam_rows, ao_count)
-    v_whole = lax.all_gather(v_coeff, "blk", axis=1, tiled=True)
+    devices = lax.axis_size("blk")
+    parts = jnp.stack([v_coeff for _ in range(devices)])
+    parts = lax.all_to_all(parts, "blk", split_axis=0, concat_axis=0)
+    v_whole = jnp.concatenate(parts, axis=1)
     half_done = jnp.dot(ints_flat, v_whole, preferred_element_type=jnp.float32).astype(jnp.bfloat16)
     half_done = half_done.reshape(sig_rows, lam_rows, -1)
     owned_rows = lax.all_to_all(half_done, "blk", split_axis=2, concat_axis=1, tiled=True)

time: 248 us -> 279 us (1.12)
  waiting for transfers between devices: 135 us -> 164 us
  between operations: 13.6 us -> 0.18 us
  starting transfers between devices: 20.8 us -> 33.6 us
    all_to_all x0 -> x1, waiting for transfers between devices: none -> 104 us  [local(): parts = lax.all_to_all(parts, 'blk', split_axis=0, concat_axis=0)]
    all_gather x1 -> x0, waiting for transfers between devices: 73.7 us -> none  [local(): v_whole = lax.all_gather(v_coeff, 'blk', axis=1, tiled=True)]
    unnamed x9, local copies, waits for them, and re-layouts: 27 us -> 10.8 us
    reshape x0 -> x2, local copies, waits for them, and re-layouts: none -> 15 us  [local(): v_whole = jnp.concatenate(parts, axis=1)]
    all_to_all x0 -> x1, starting transfers between devices: none -> 10.4 us  [local(): parts = lax.all_to_all(parts, 'blk', split_axis=0, concat_axis=0)]
    another operation x0 -> x1, local copies, waits for them, and re-layouts: none -> 3.6 us  [local(): parts = jnp.stack([v_coeff for _ in range(devices)])]
  transfers between devices with their start and end apart: 4 -> 4, of which waited for: 4 -> 4; matrix products, arithmetic and copies ran while one was open for 5% -> 4% of each run, Pallas kernels for 0% -> 0%
where the time goes in v1:
time: 279 us; the launch traced here: 278 us
  waiting for transfers between devices  164 us (59%)
  local copies, waits for them, and re-layouts  67.9 us (24%)
  starting transfers between devices  33.6 us (12%)
  matrix products  9.71 us (3%)
    all_to_all x1, waiting for transfers between devices, local(): parts = lax.all_to_all(parts, 'blk', split_axis=0, concat_axis=0)  104 us
    all_to_all x2, waiting for transfers between devices, several_exchanges(): lax.all_to_all(section, axis, split_axis=0, concat_axis=0, tiled=True)  39.7 us
    all_to_all x1, waiting for transfers between devices, local(): lax.all_to_all(half_done, 'blk', split_axis=2, concat_axis=1, tiled=True)  20.5 us
    reshape x2, local copies, waits for them, and re-layouts, local(): v_whole = jnp.concatenate(parts, axis=1)  15 us
    all_to_all x2, starting transfers between devices, several_exchanges(): lax.all_to_all(section, axis, split_axis=0, concat_axis=0, tiled=True)  14.5 us
    reshape x2, local copies, waits for them, and re-layouts, local(): blocked = third_done.reshape(sig_rows, a_local, block_count, block_width)  13.9 us
    unnamed x9, local copies, waits for them, and re-layouts  10.8 us
    all_to_all x1, starting transfers between devices, local(): parts = lax.all_to_all(parts, 'blk', split_axis=0, concat_axis=0)  10.4 us
  transfers between devices with their start and end apart: 4, of which 4 were waited for; matrix products, arithmetic and copies ran while one was open for 4% of the time, Pallas kernels for 0%

profile of v1, /device:TPU:8, one launch (start us, length us, event | category | flops | bytes accessed | tf_op | source)
XLA Modules:
  0.0 278.4 jit_solution(2905086653241300545)
XLA Ops:
  0.0 3.6 %stack.2 = bf16[32,1504,42]{1,2,0:T(8,128)(2,1)} broadcast(bf16[1504,42]{0,1:T(8,128)(2,1)} %param.5), dimensions={1,2} | broadcast | bytes 4169088 | tf_op jit(solution)/shard_map/stack | solution.py:37
  3.6 0.0 copy-start
  3.6 10.4 %all-to-all-start = ((bf16[32,1504,42]{1,2,0:T(8,128)(2,1)}), bf16[32,1504,42]{1,2,0:T(8,128)(2,1)}, u32[]{:S(2)}, u32[]{:S(2)}) async-start(bf16[32,1504,42]{1,2,0:T(8,128)(2,1)} %stack.2), calls=%async_computation | async-start | bytes 9437184 | tf_op jit(solution)/shard_map/all_to_all | solution.py:38
  14.0 0.0 copy-done
  14.0 0.3 copy.37
  14.3 0.5 reshape.51
  14.9 104.1 %all-to-all-done = bf16[32,1504,42]{1,2,0:T(8,128)(2,1)} async-done(((bf16[32,1504,42]{1,2,0:T(8,128)(2,1)}), bf16[32,1504,42]{1,2,0:T(8,128)(2,1)}, u32[]{:S(2)}, u32[]{:S(2)}) %all-to-all-start) | async-done | bytes 4042784 | tf_op jit(solution)/shard_map/all_to_all | solution.py:38
  118.9 7.5 %reshape.53 = bf16[1504,1344]{0,1:T(8,128)(2,1)} reshape(bf16[1504,32,42]{0,2,1:T(8,128)(2,1)} %bitcast) | data formatting | bytes 8085504 | tf_op jit(solution)/shard_map/reshape | solution.py:39
  126.4 5.5 %convolution_convert_fusion.1 = bf16[376,1344]{0,1:T(8,128)(2,1)} fusion(bf16[376,1504]{1,0:T(8,128)(2,1)S(1)} %reshape.51, bf16[1504,1344]{0,1:T(8,128)(2,1)} %reshape.53), kind=kOutput, calls=%fused_computation.3 | convolution fusion | flops 1520580096 | bytes 6184448 | tf_op jit(solution)/shard_map/dot_general | solution.py:40
  131.9 3.8 %reshape.74 = bf16[8,47,1344]{1,0,2:T(8,128)(2,1)S(1)} reshape(bf16[376,1344]{0,1:T(8,128)(2,1)} %convolution_convert_fusion.1) | data formatting | bytes 2021376 | tf_op jit(solution)/shard_map/reshape | solution.py:41
  135.8 4.9 %reshape.78 = bf16[32,2,7896]{2,1,0:T(2,128)(2,1)} reshape(bf16[1344,8,47]{2,1,0:T(8,128)(2,1)S(1)} %bitcast.33) | data formatting | bytes 2021376
  140.7 0.0 copy-start.1
  140.7 8.7 %all-to-all-start.1 = ((bf16[32,2,7896]{2,1,0:T(2,128)(2,1)}), bf16[32,2,7896]{2,1,0:T(2,128)(2,1)}, u32[]{:S(2)}, u32[]{:S(2)}) async-start(bf16[32,2,7896]{2,1,0:T(2,128)(2,1)} %reshape.78), calls=%async_computation.1 | async-start | bytes 2031616 | tf_op jit(solution)/shard_map/all_to_all | solution.py:42
  149.4 0.0 copy-done.1
  149.4 0.1 broadcast_in_dim.40
  149.5 0.1 broadcast_in_dim.41
  149.6 0.1 broadcast_in_dim.42
  149.7 7.5 %reshape.73 = bf16[1504,1344,1]{0,1,2:T(8,128)(2,1)} reshape(bf16[1504,32,42]{0,2,1:T(8,128)(2,1)} %bitcast) | data formatting | bytes 8085504 | tf_op jit(solution)/shard_map/reshape | solution.py:39
  157.2 20.5 %all-to-all-done.1 = bf16[32,2,7896]{2,1,0:T(2,128)(2,1)} async-done(((bf16[32,2,7896]{2,1,0:T(2,128)(2,1)}), bf16[32,2,7896]{2,1,0:T(2,128)(2,1)}, u32[]{:S(2)}, u32[]{:S(2)}) %all-to-all-start.1) | async-done | bytes 1010720 | tf_op jit(solution)/shard_map/all_to_all | solution.py:42
  177.7 5.5 %reshape.79 = bf16[1344,8,47]{2,1,0:T(8,128)(2,1)S(1)} reshape(bf16[32,2,7896]{2,1,0:T(2,128)(2,1)} %all-to-all-done.1) | data formatting | bytes 2021376
  183.3 2.3 copy.51
  185.5 5.7 %reshape.75 = bf16[8,1504,42]{1,2,0:T(8,128)(2,1)S(1)} reshape(bf16[8,32,47,42]{2,1,3,0:T(8,128)(2,1)} %copy.51) | data formatting | bytes 2021376 | tf_op jit(solution)/shard_map/all_to_all | solution.py:42
  191.2 4.2 %convolution_convert_fusion = bf16[8,42,1344]{2,1,0:T(8,128)(2,1)S(1)} fusion(bf16[8,1504,42]{1,2,0:T(8,128)(2,1)S(1)} %reshape.75, bf16[1504,1344,1]{0,1,2:T(8,128)(2,1)} %reshape.73), kind=kOutput, calls=%fused_computation.2 | convolution fusion | flops 1358816256 | bytes 5956608 | tf_op jit(solution)/shard_map/dot_general | solution.py:43
  195.4 8.9 %reshape.77 = bf16[8,42,32,42]{3,2,1,0:T(8,128)(2,1)} reshape(bf16[8,42,1344]{2,1,0:T(8,128)(2,1)S(1)} %convolution_convert_fusion) | data formatting | bytes 1806336 | tf_op jit(solution)/shard_map/reshape | solution.py:49
  204.3 5.0 %copy.44 = bf16[8,42,32,42]{3,0,2,1:T(8,128)(2,1)S(1)} copy(bf16[8,42,32,42]{3,2,1,0:T(8,128)(2,1)} %reshape.77) | data formatting | bytes 1806336 | tf_op jit(solution)/shard_map/reshape | solution.py:49
  209.3 3.0 %gather_fusion = bf16[32,8,42,42]{3,1,2,0:T(8,128)(2,1)} fusion(bf16[8,42,32,42]{3,0,2,1:T(8,128)(2,1)S(1)} %copy.44, s32[1024]{0:T(1024)S(1)} %pad_clamp_fusion.1), kind=kCustom, calls=%fused_computation | custom fusion | bytes 1806464 | tf_op jit(solution)/shard_map/jit(_take)/gather | solution.py:50
  212.3 2.5 copy.45
  214.7 2.4 gather.13
  217.1 1.8 fusion
  218.9 0.8 split.8
  219.8 10.9 %all-to-all-start.2 = ((bf16[16,8,16,84]{3,1,2,0:T(8,128)(2,1)}), bf16[16,8,16,84]{3,1,2,0:T(8,128)(2,1)S(1)}, u32[]{:S(2)}, u32[]{:S(2)}) async-start(bf16[16,8,16,84]{3,1,2,0:T(8,128)(2,1)} %split.8), calls=%async_computation.2 | async-start | bytes 1048576 | tf_op jit(solution)/shard_map/all_to_all | solution.py:29
  230.7 0.0 copy-start.2
  230.7 1.0 split.9
  231.7 16.7 %all-to-all-done.2 = bf16[16,8,16,84]{3,1,2,0:T(8,128)(2,1)S(1)} async-done(((bf16[16,8,16,84]{3,1,2,0:T(8,128)(2,1)}), bf16[16,8,16,84]{3,1,2,0:T(8,128)(2,1)S(1)}, u32[]{:S(2)}, u32[]{:S(2)}) %all-to-all-start.2) | async-done | bytes 344096 | tf_op jit(solution)/shard_map/all_to_all | solution.py:29
  248.4 3.6 %all-to-all-start.3 = ((bf16[16,8,26,84]{3,1,2,0:T(8,128)(2,1)}), bf16[16,8,26,84]{3,1,2,0:T(8,128)(2,1)S(1)}, u32[]{:S(2)}, u32[]{:S(2)}) async-start(bf16[16,8,26,84]{3,1,2,0:T(8,128)(2,1)} %split.9), calls=%async_computation.3 | async-start | bytes 1703936 | tf_op jit(solution)/shard_map/all_to_all | solution.py:29
  252.0 0.0 copy-done.2
  252.0 0.2 convert_reduce_fusion
  252.2 0.1 select_reduce_fusion
  252.3 0.1 broadcast_in_dim.37
  252.4 0.1 broadcast_in_dim.38
  252.5 23.0 %all-to-all-done.3 = bf16[16,8,26,84]{3,1,2,0:T(8,128)(2,1)S(1)} async-done(((bf16[16,8,26,84]{3,1,2,0:T(8,128)(2,1)}), bf16[16,8,26,84]{3,1,2,0:T(8,128)(2,1)S(1)}, u32[]{:S(2)}, u32[]{:S(2)}) %all-to-all-start.3) | async-done | bytes 559136 | tf_op jit(solution)/shard_map/all_to_all | solution.py:29
  275.6 0.3 pad_maximum_fusion
  275.8 0.8 gather_fusion.1
  276.6 0.2 bitcast_select_fusion
  276.9 1.5 copy.48
  (6 shorter events, 0.0 us)
Async XLA Ops:
  3.6 10.4 %copy-start = (bf16[8,47,1504]{2,0,1:T(8,128)(2,1)S(1)}, bf16[8,47,1504]{2,0,1:T(8,128)(2,1)}, u32[]{:S(2)}) copy-start(bf16[8,47,1504]{2,0,1:T(8,128)(2,1)} %param.4) | copy-start | bytes 3393028
  3.6 115.3 %all-to-all-start = ((bf16[32,1504,42]{1,2,0:T(8,128)(2,1)}), bf16[32,1504,42]{1,2,0:T(8,128)(2,1)}, u32[]{:S(2)}, u32[]{:S(2)}) async-start(bf16[32,1504,42]{1,2,0:T(8,128)(2,1)} %stack.2), calls=%async_computation | async-start | bytes 9437184 | tf_op jit(solution)/shard_map/all_to_all | solution.py:38
  140.7 8.7 %copy-start.1 = (s32[32]{0:T(128)S(1)}, s32[32]{0:T(128)}, u32[]{:S(2)}) copy-start(s32[32]{0:T(128)} %param.7) | copy-start | bytes 388
  140.7 37.0 %all-to-all-start.1 = ((bf16[32,2,7896]{2,1,0:T(2,128)(2,1)}), bf16[32,2,7896]{2,1,0:T(2,128)(2,1)}, u32[]{:S(2)}, u32[]{:S(2)}) async-start(bf16[32,2,7896]{2,1,0:T(2,128)(2,1)} %reshape.78), calls=%async_computation.1 | async-start | bytes 2031616 | tf_op jit(solution)/shard_map/all_to_all | solution.py:42
  219.8 28.6 %all-to-all-start.2 = ((bf16[16,8,16,84]{3,1,2,0:T(8,128)(2,1)}), bf16[16,8,16,84]{3,1,2,0:T(8,128)(2,1)S(1)}, u32[]{:S(2)}, u32[]{:S(2)}) async-start(bf16[16,8,16,84]{3,1,2,0:T(8,128)(2,1)} %split.8), calls=%async_computation.2 | async-start | bytes 1048576 | tf_op jit(solution)/shard_map/all_to_all | solution.py:29
  230.7 21.3 %copy-start.2 = (s32[16]{0:T(128)S(1)}, s32[16]{0:T(128)}, u32[]{:S(2)}) copy-start(s32[16]{0:T(128)} %param.6) | copy-start | bytes 196
  248.4 27.2 %all-to-all-start.3 = ((bf16[16,8,26,84]{3,1,2,0:T(8,128)(2,1)}), bf16[16,8,26,84]{3,1,2,0:T(8,128)(2,1)S(1)}, u32[]{:S(2)}, u32[]{:S(2)}) async-start(bf16[16,8,26,84]{3,1,2,0:T(8,128)(2,1)} %split.9), calls=%async_computation.3 | async-start | bytes 1703936 | tf_op jit(solution)/shard_map/all_to_all | solution.py:29
